TPU v7x, 32 devices: a whole 2x2x4 slice. The times are simulated.
32 devices in a mesh: apa: 2 (over y), gz: 4 (over x, core), drift: 4 (over z).
Axes of the slice: x: 2, y: 2, z: 4, core: 2. Of those that a mesh axis runs over, the one named last changes fastest.
Arguments:
- charge: bfloat16 [16384, 384], P(('apa', 'gz', 'drift')), parts along dimension 0, may hold values from 0.049804688 to 2
- intersection: bfloat16 [128, 3, 2, 32, 128], P(('apa', 'gz', 'drift')), parts along dimension 0, may hold values from 0 to 0.03125
- ovl_block: int32 [128, 3, 2], P(('apa', 'gz', 'drift')), parts along dimension 0, may hold values from 0 to 15, as said below
- ovl_count: int32 [128, 3], P(('apa', 'gz', 'drift')), parts along dimension 0, may hold values from 1 to 2
- diff_class: int32 [768], P('apa'), parts along dimension 0, may hold values from 0 to 5
- response: bfloat16 [3, 21, 200], replicated, may hold values from -0.029907227 to 0.029907227
- cotangent: bfloat16 [6, 512, 3072], P('apa', 'gz', 'drift'), parts along dimension 0, may hold values from -120 to 120
Outputs:
- signal: bfloat16 [6, 512, 3072], P('apa', 'gz', 'drift'), parts along dimension 0
- charge_grad: bfloat16 [16384, 384], P(('apa', 'gz', 'drift')), parts along dimension 0
There are 2 independent parts, one for each index of `apa`. A program takes and returns all parts, laid end to end along the dimension named above; an argument that names none is the same for every part. Nothing has to cross between parts.
Inputs may be any that keep to these rules, and one draw needn't show every extreme that they name: `ovl_block`: planes are U, V, W in this order. Cell block b lies in z-block b // 16; its W entries name wire blocks of that z-block, z-block g owning wire blocks g * 4 to (g + 1) * 4 - 1 of every plane. Entry 0 of each list is live. Among the live U and V entries of one group of 4 consecutive cell blocks (starting at a multiple of 4), at most 8 name wire blocks of one z-block, and every such group reaches 8 for some z-block. `ovl_count`: entry k of a list is live where k < count; the others are ignored.
All inputs are finite; a program needn't handle non-finite values.
Results may differ from a plain program's by a relative error of at most 0.0058.
Values may be sent and summed in bfloat16 or wider, within the bound.
A program may use at most 128 MiB of HBM per device.

v0:
```python
import functools
import math

import jax
import jax.numpy as jnp
from jax import lax
from jax.experimental import pallas as pl
from jax.experimental.pallas import tpu as pltpu
from jax.sharding import PartitionSpec as P

TPB = 8
HB = 2
LIMIT = 44
LANES = 128
ROWS = 16
WIN = 64
NDIFF = 6
MESH = pl.DeviceIdType.MESH
F32 = jnp.float32
BF16 = jnp.bfloat16

VMEM = pl.BlockSpec(memory_space=pltpu.VMEM)
SMEM = pl.BlockSpec(memory_space=pltpu.SMEM)
HBM = pl.BlockSpec(memory_space=pltpu.HBM)

REACH = HB * TPB
LOW = -(REACH - (TPB - 1) // 2 - 1)


def round_up(value, step):
    return -(-value // step) * step


def iota(shape, dim):
    return lax.broadcasted_iota(jnp.int32, shape, dim)


def dot(left, right, contract=((1,), (0,))):
    return lax.dot_general(left, right, (contract, ((), ())), preferred_element_type=F32)


def class_scale(k):
    width = TPB * (0.2 + 0.15 * k)
    return 1.0 / (2.0 * width * width)


def class_norm(k):
    return sum(math.exp(-((j + 0.5) ** 2) * class_scale(k)) for j in range(-REACH, REACH))


def kernel(
    cfg,
    blk_hbm,
    cnt_hbm,
    charge_hbm,
    inter_hbm,
    class_hbm,
    resp_hbm,
    cot_hbm,
    sig_ref,
    grad_ref,
    blk_ref,
    cnt_ref,
    charge_ref,
    inter_ref,
    class_ref,
    resp_ref,
    cot_ref,
    load_s,
    round_s,
    spread_ref,
    own_ref,
    csend_ref,
    crecv_ref,
    xsend_ref,
    xrecv_ref,
    place_ref,
    zsend_ref,
    zrecv_ref,
    zgate_ref,
    zsum_ref,
    hrecv_ref,
    chalo_ref,
    every_ref,
    spread_t_ref,
    taps_ref,
    table_ref,
    green_ref,
    wide_ref,
    field_ref,
    pair_ref,
    total_ref,
    core_s,
    core_r,
    x_s,
    x_r,
    z_s,
    z_r,
    zg_r,
    h_s,
    h_r,
    c_s,
    c_r,
    ga_r,
    gr_s,
    gx_s,
    gx_r,
    gc_s,
):
    owners, slabs, front, pairs, block = cfg
    blocks, planes, entries, wires, cells = inter_ref.shape
    bins = charge_ref.shape[1]
    here, ticks_here = cot_ref.shape[1:]
    spread, length = resp_ref.shape[1:]
    per_owner = here // wires
    bins_here = bins // slabs
    half = (spread - 1) // 2
    chips = owners // 2
    rows = 2 * here
    chunks = ticks_here // block
    slots = 2 * pairs

    z = lax.axis_index("drift")
    g = lax.axis_index("gz")
    core = g % 2
    chip = g // 2
    partner = g + 1 - 2 * core

    def remote(src, dst, send, recv, gz, drift):
        return pltpu.make_async_remote_copy(
            src_ref=src,
            dst_ref=dst,
            send_sem=send,
            recv_sem=recv,
            device_id={"gz": gz, "drift": drift},
            device_id_type=MESH,
        )

    loads = [
        pltpu.make_async_copy(src, dst, load_s.at[n])
        for n, (src, dst) in enumerate(
            (
                (blk_hbm, blk_ref),
                (cnt_hbm, cnt_ref),
                (inter_hbm, inter_ref),
                (charge_hbm, charge_ref),
                (class_hbm, class_ref),
                (resp_hbm, resp_ref),
                (cot_hbm, cot_ref),
            )
        )
    ]
    for load in loads:
        load.start()

    barrier = pltpu.get_barrier_semaphore()

    def greet(sem, gz, drift):
        pl.semaphore_signal(
            sem, inc=1, device_id={"gz": gz, "drift": drift}, device_id_type=MESH
        )

    has_prev = g > 0
    has_next = g < owners - 1
    sides = has_prev.astype(jnp.int32) + has_next.astype(jnp.int32)
    has_left = z > 0
    has_right = z < slabs - 1
    rounds = chips == 2 and slabs <= 4

    def near(sem):
        for j in range(1, chips):
            greet(sem, ((chip + j) % chips) * 2 + core, z)
        if rounds:

            @pl.when(has_left)
            def _():
                greet(sem, g, z - 1)

            @pl.when(has_right)
            def _():
                greet(sem, g, z + 1)

        else:
            for j in range(1, slabs):
                greet(sem, g, (z + j) % slabs)
        here_only = [z] if rounds else list(range(slabs))

        @pl.when(has_prev)
        def _():
            for d in here_only:
                greet(sem, g - 1, d)

        @pl.when(has_next)
        def _():
            for d in here_only:
                greet(sem, g + 1, d)

    ends = has_left.astype(jnp.int32) + has_right.astype(jnp.int32)
    if rounds:
        near_count = (chips - 1) + ends + sides
    else:
        near_count = (chips - 1) + (slabs - 1) + slabs * sides
    near(barrier)

    def second_round():
        if rounds:
            near(round_s.at[0])

    def third_round():
        if rounds:
            pl.semaphore_wait(round_s.at[0], near_count)
            for step in (1, 2):

                @pl.when(z >= step)
                def _():
                    greet(round_s.at[1], g, z - step)

                @pl.when(z + step < slabs)
                def _():
                    greet(round_s.at[1], g, z + step)

    def all_here():
        if rounds:
            count = 0
            for step in (1, 2):
                count += (z >= step).astype(jnp.int32) + (z + step < slabs).astype(jnp.int32)
            pl.semaphore_wait(round_s.at[1], count)

    for load in loads[:3]:
        load.wait()
    def spread_block(block_index, p, at):
        for b in range(blocks):
            total = jnp.zeros((wires, cells), BF16)
            for k in range(entries):
                named = (blk_ref[p, k, b] == block_index) & (k < cnt_ref[b, p])
                total = total + jnp.where(named, inter_ref[b, p, k], jnp.zeros((wires, cells), BF16))
            spread_ref[pl.ds(at, wires), b * cells : (b + 1) * cells] = total

    def spread_owner(owner, _):
        for p in range(2):
            for q in range(per_owner):
                spread_block(
                    owner * per_owner + q,
                    p,
                    pl.multiple_of(owner * rows + (p * per_owner + q) * wires, wires),
                )
        return 0

    lax.fori_loop(0, owners, spread_owner, 0)
    for q in range(per_owner):
        spread_block(g * per_owner + q, 2, owners * rows + q * wires)

    loads[3].wait()
    charge = charge_ref[...]
    for k in range(chips):
        there = pl.multiple_of((2 * k + 1 - core) * rows, rows)
        csend_ref[k] = dot(spread_ref[pl.ds(there, rows), :], charge).astype(BF16)

    depth = round_up(length, ROWS)
    loads[4].wait()
    loads[5].wait()
    taps_ref[...] = jnp.zeros_like(taps_ref)
    for p in range(planes):
        taps_ref[p, 0:spread, 0:length] = resp_ref[p].astype(F32)
    taps = taps_ref[...].reshape(planes * taps_ref.shape[1], taps_ref.shape[2]).astype(BF16)
    row_class = class_ref[...].reshape(1, bins)
    tables = NDIFF + 2
    delta = iota((depth, 2 * LANES), 1) - iota((depth, 2 * LANES), 0)
    offset = (delta + LOW).astype(F32) - (TPB - 1) / 2
    inside = jnp.abs(offset) < REACH
    squared = offset * offset
    for k in range(tables):
        if k < NDIFF:
            scale, norm = class_scale(k), class_norm(k)
            keep = inside
        else:
            first = row_class[:, k - NDIFF : k - NDIFF + 1]
            scale = jnp.zeros((1, 1), F32)
            norm = jnp.zeros((1, 1), F32)
            for c in range(NDIFF):
                scale += jnp.where(first == c, class_scale(c), 0.0)
                norm += jnp.where(first == c, class_norm(c), 0.0)
            keep = inside & (delta + LOW + TPB * (k - NDIFF) >= 0)
        smear = jnp.where(keep, jnp.exp(-squared * scale), 0.0) / norm
        upper = smear.astype(BF16)
        lower = (smear - upper.astype(F32)).astype(BF16)
        spot = pl.ds(k, taps.shape[0], stride=tables)
        filtered = dot(taps, upper) + dot(taps, lower)
        table_ref[0, spot, :] = filtered[:, :LANES]
        table_ref[1, spot, :] = filtered[:, LANES:]

    bin_of = iota((LANES, bins), 0) + bins_here * z - front
    chosen = jnp.where(iota((LANES, bins), 1) == bin_of, 1.0, 0.0).astype(BF16)
    bin_row = iota((tables, bins), 1)
    table_row = iota((tables, bins), 0)
    wanted = jnp.where(bin_row < 2, NDIFF + bin_row, row_class)
    uses = jnp.where(table_row == wanted, 1.0, 0.0).astype(BF16)
    pick = dot(chosen, uses, ((1,), (1,))).astype(BF16)

    start = (LOW - TPB * front) % LANES
    blocks_of = LANES // TPB
    turn = iota((LANES, LANES), 0) % blocks_of * TPB + start
    right = iota((LANES, LANES), 1) >= turn
    group = slots // 2

    def split(value):
        upper = value.astype(BF16)
        return upper, (value - upper.astype(F32)).astype(BF16)

    def green_rows(p, part, step):
        j0 = step * group
        for u in range(group):
            j = j0 + u
            at = pl.multiple_of((p * taps_ref.shape[1] + j) * tables, tables)
            one, two = (
                pltpu.roll(
                    dot(pick, split(table_ref[n, pl.ds(at, tables), :])[part]),
                    start,
                    1,
                    stride=TPB,
                    stride_axis=0,
                )
                for n in range(2)
            )
            outs = (
                jnp.where(right, one, 0.0).astype(BF16),
                jnp.where(right, two, one).astype(BF16),
                jnp.where(right, 0.0, two).astype(BF16),
                jnp.zeros((LANES, LANES), BF16),
            )
            for q in range(LANES // blocks_of):
                here_rows = slice(q * blocks_of, (q + 1) * blocks_of)
                base = q - (TPB * front - LOW + start) // LANES
                for n in range(4):
                    lanes = (base + n) % 4 * LANES
                    green_ref[part, p, j, here_rows, lanes : lanes + LANES] = outs[n][here_rows]

    def green(p, part):
        def half_of(step, _):
            green_rows(p, part, step)
            return 0

        lax.fori_loop(0, 2, half_of, 0)

    def operator(p, c, half_of=0):
        first = block * c // TPB
        lanes = block * c % (4 * LANES)
        part = green_ref[half_of, p, :, first : first + WIN, lanes : lanes + block]
        return part.reshape(slots * WIN, block)

    pl.semaphore_wait(barrier, near_count)
    second_round()

    def core_copy(k):
        return remote(
            csend_ref.at[k], crecv_ref.at[k], core_s.at[k], core_r.at[k], partner, z
        )

    for j in range(1, chips + 1):
        core_copy((chip + j) % chips).start()

    def cot_down():
        return remote(
            cot_hbm.at[:, 0:ROWS], chalo_ref.at[1], c_s.at[1], c_r.at[1], g - 1, z
        )

    def cot_up():
        return remote(
            cot_hbm.at[:, here - ROWS : here], chalo_ref.at[0], c_s.at[0], c_r.at[0], g + 1, z
        )

    @pl.when(has_prev)
    def _():
        cot_down().start()

    @pl.when(has_next)
    def _():
        cot_up().start()

    @pl.when(g == 0)
    def _():
        chalo_ref[0] = jnp.zeros(chalo_ref.shape[1:], BF16)
        hrecv_ref[0] = jnp.zeros(hrecv_ref.shape[1:], BF16)

    @pl.when(g == owners - 1)
    def _():
        chalo_ref[1] = jnp.zeros(chalo_ref.shape[1:], BF16)
        hrecv_ref[1] = jnp.zeros(hrecv_ref.shape[1:], BF16)

    lane = iota((bins, slabs * LANES), 1)
    place_ref[...] = jnp.where(
        iota((bins, slabs * LANES), 0)
        == (lane // LANES) * bins_here - front + lane % LANES,
        1.0,
        0.0,
    ).astype(BF16)

    mid = slabs // 2
    low_half = z < mid
    base = jnp.where(low_half, 0, mid)
    base_there = mid - base
    gate = jnp.where(low_half, mid - 1, mid)
    gate_there = slabs - 1 - gate
    is_gate = z == gate

    def in_half(j):
        return base + (z - base + j) % mid

    def frame(p, sums):
        framed = dot(sums.astype(BF16), place_ref[...]).astype(BF16)
        for d in range(slabs):
            zsend_ref[d, p] = framed[:, d * LANES : (d + 1) * LANES]

    def half_copy(j, p):
        return remote(
            zsend_ref.at[in_half(j), p],
            zrecv_ref.at[j - 1, p],
            z_s.at[0],
            z_r.at[j - 1, p],
            g,
            in_half(j),
        )

    giver = jnp.where(low_half, z, z - mid - 1)

    def gate_copy(i, p):
        return remote(
            zsend_ref.at[base_there + i, p],
            zgate_ref.at[jnp.clip(giver, 0, mid - 2), i, p],
            z_s.at[1],
            zg_r.at[jnp.clip(giver, 0, mid - 2), p],
            g,
            gate,
        )

    def arrived(ref, sem):
        remote(ref, ref, z_s.at[0], sem, g, z).wait_recv()

    def sent(ref, sem):
        remote(ref, ref, sem, z_r.at[0, 0], g, z).wait_send()

    def sum_copy(i, p):
        return remote(
            zsum_ref.at[i, p],
            zrecv_ref.at[mid - 1, p],
            z_s.at[2],
            z_r.at[mid - 1, p],
            g,
            base_there + i,
        )

    def edge_copy(side, j, p):
        rows_of = slice(here - ROWS, here) if side == 0 else slice(0, ROWS)
        return remote(
            zsend_ref.at[in_half(j), p, rows_of],
            hrecv_ref.at[side, j, p],
            h_s.at[side],
            h_r.at[side, p],
            g + 1 if side == 0 else g - 1,
            in_half(j),
        )

    def edge_sum(side, i, p):
        rows_of = slice(here - ROWS, here) if side == 0 else slice(0, ROWS)
        return remote(
            zsum_ref.at[i, p, rows_of],
            hrecv_ref.at[side, mid, p],
            h_s.at[2 + side],
            h_r.at[side, p],
            g + 1 if side == 0 else g - 1,
            base_there + i,
        )

    def edges(side):
        return has_next if side == 0 else has_prev

    def send_windows(p):
        @pl.when(jnp.logical_not(is_gate))
        def _():
            for i in range(mid):
                gate_copy(i, p).start()

        for j in range(1, mid):
            half_copy(j, p).start()
        for side in range(2):

            @pl.when(edges(side))
            def _():
                for j in range(mid):
                    edge_copy(side, j, p).start()

    def gate_sums(p):
        @pl.when(is_gate)
        def _():
            for n in range(mid - 1):
                arrived(zgate_ref.at[n, :, p], zg_r.at[n, p])
            for i in range(mid):
                total = zsend_ref[base_there + i, p].astype(F32)
                for n in range(mid - 1):
                    total += zgate_ref[n, i, p].astype(F32)
                zsum_ref[i, p] = total.astype(BF16)
                sum_copy(i, p).start()
            for side in range(2):

                @pl.when(edges(side))
                def _():
                    for i in range(mid):
                        edge_sum(side, i, p).start()

    def own_parts():
        frame(2, dot(spread_ref[owners * rows : owners * rows + here, :], charge))
        for k in range(chips):
            there = pl.multiple_of((2 * k + core) * rows, rows)
            own_ref[k] = dot(spread_ref[pl.ds(there, rows), :], charge)

    turned = here % LANES == 0

    def turn_shares():
        if turned:
            for n in range(spread_ref.shape[0] // LANES):
                part = slice(n * LANES, (n + 1) * LANES)
                spread_t_ref[:, part] = spread_ref[part, :].T

    def x_copy(j, p):
        return remote(
            xsend_ref.at[j - 1, p],
            xrecv_ref.at[j - 1, p],
            x_s.at[j - 1, p],
            x_r.at[j - 1, p],
            ((chip + j) % chips) * 2 + core,
            z,
        )

    def core_sums():
        for j in range(1, chips):
            k = (chip + j) % chips
            core_copy(k).wait_recv()
            for p in range(2):
                part = pl.ds(p * here, here)
                xsend_ref[j - 1, p] = (
                    own_ref[k, part, :] + crecv_ref[k, part, :].astype(F32)
                ).astype(BF16)
                x_copy(j, p).start()

    def place_of(owner, p):
        at = owner * rows + p * here if p < 2 else owners * rows
        return pl.ds(pl.multiple_of(at, here), here)

    def block_at(d, owner, p):
        return every_ref.at[d, place_of(owner, p)]

    def ag_copy(j, p):
        part = block_at(z, g, p)
        to = in_half(j) if j else gate_there
        return remote(part, part, z_s.at[3], ga_r.at[z, p], g, to)

    def ag_pass(i, j, p):
        d = base_there + i
        part = block_at(d, g, p)
        return remote(part, part, gr_s.at[j - 1], ga_r.at[d, p], g, in_half(j))

    def ag_wait(d, p):
        part = block_at(d, g, p)
        arrived(part, ga_r.at[d, p])

    def gx_copy(j, d, p, owner):
        part = block_at(d, owner, p)
        return remote(
            part,
            part,
            gx_s.at[j - 1],
            gx_r.at[j - 1, d, p],
            ((chip + j) % chips) * 2 + core,
            z,
        )

    def gc_copy(d, p, owner):
        part = block_at(d, owner, p)
        return remote(part, part, gc_s.at[0], gc_s.at[1], partner, z)

    def spread_bins(d, p):
        if p < 2:
            for j in range(1, chips):
                gx_copy(j, d, p, g).start()
            gc_copy(d, p, g).start()

    def relay(p):
        @pl.when(is_gate)
        def _():
            for i in range(mid):
                ag_wait(base_there + i, p)
                for j in range(1, mid):
                    ag_pass(i, j, p).start()
                spread_bins(base_there + i, p)

    def far_bins(p):
        @pl.when(jnp.logical_not(is_gate))
        def _():
            for i in range(mid):
                ag_wait(base_there + i, p)
                spread_bins(base_there + i, p)

    def near_bins(p):
        for j in range(1, mid):
            ag_wait(in_half(j), p)
            spread_bins(in_half(j), p)

    def pass_bins(p):
        for d in range(slabs):
            for j in range(1, chips):
                owner = ((chip - j) % chips) * 2 + core
                gx_copy(j, d, p, owner).wait_recv()
                gc_copy(d, p, owner).start()

    def core_bins():
        arrived(every_ref.at[:, 0 : chips * rows], gc_s.at[1])

    column = iota((here, LANES), 1)

    def backward(p):
        total = jnp.zeros((here, LANES), F32)
        for c in range(chunks):
            ticks = slice(c * block, (c + 1) * block)
            data = jnp.concatenate(
                [chalo_ref[0, p, :, ticks], cot_ref[p, :, ticks], chalo_ref[1, p, :, ticks]], 0
            )
            wide_ref[...] = dot(data, operator(p, c), ((1,), (1,)))
            low = jnp.zeros((here, LANES), F32)
            high = jnp.zeros((here, LANES), F32)
            for m in range(pairs):
                lanes = slice(m * LANES, (m + 1) * LANES)
                at = ROWS + half - 2 * m
                low += wide_ref[at : at + here, lanes]
                if 2 * m + 1 < spread:
                    high += wide_ref[at - 1 : at - 1 + here, lanes]
            first = block * c // TPB
            low = jnp.where(column < WIN, low, 0.0)
            high = jnp.where(column < WIN, 0.0, high)
            if first:
                low = pltpu.roll(low, first, 1)
            total += low + pltpu.roll(high, (WIN + first) % LANES, 1)
        every_ref[z, place_of(g, p), :] = total.astype(BF16)
        for j in range(mid):
            ag_copy(j, p).start()

    def sum_and_send(p):
        part = pl.ds(p * here, here)
        sums = own_ref[chip, part, :] + crecv_ref[chip, part, :].astype(F32)
        for j in range(1, chips):
            x_copy(j, p).wait_recv()
            sums += xrecv_ref[j - 1, p].astype(F32)
        frame(p, sums)
        send_windows(p)

    def window_sum(p):
        total = zsend_ref[z, p].astype(F32)
        for j in range(1, mid):
            half_copy(j, p).wait_recv()
            total += zrecv_ref[j - 1, p].astype(F32)
        sum_copy(0, p).wait_recv()
        total += zrecv_ref[mid - 1, p].astype(F32)
        field_ref[p, ROWS : ROWS + here, :] = total

    tall = here + 2 * ROWS
    used = tall

    def forward(p):
        window_sum(p)

        for side in range(2):

            @pl.when(has_prev if side == 0 else has_next)
            def _():
                arrived(hrecv_ref.at[side, :, p], h_r.at[side, p])

        for side, at in ((0, 0), (1, ROWS + here)):
            edge = hrecv_ref[side, 0, p].astype(F32)
            for j in range(1, mid + 1):
                edge += hrecv_ref[side, j, p].astype(F32)
            field_ref[p, at : at + ROWS, :] = edge
        for c in range(chunks):
            first = block * c // TPB
            this = field_ref[p, 0:used, :]
            following = field_ref[p, 1 : used + 1, :]
            if first:
                this = pltpu.roll(this, LANES - first, 1)
            following = pltpu.roll(following, (WIN - first) % LANES, 1)
            pair_ref[...] = jnp.where(iota((used, LANES), 1) < WIN, this, following)
            at = ROWS - half
            taken = [split(pair_ref[at + 2 * m : at + 2 * m + here, :]) for m in range(pairs)]
            upper, lower = (jnp.concatenate([t[n] for t in taken], 1) for n in range(2))
            both = dot(jnp.concatenate([upper, lower], 0), operator(p, c))
            total = both[:here] + both[here:] + dot(upper, operator(p, c, 1))
            sig_ref[p, :, c * block : (c + 1) * block] = total.astype(BF16)

    def windows_of(part):
        return jnp.concatenate([every_ref[d, part, :] for d in range(slabs)], 1)

    def shares(part, right):
        if turned:
            return dot(spread_t_ref[:, part], right)
        return dot(spread_ref[part, :], right, ((0,), (0,)))

    def grads(owner_core, extra):
        total = None
        for k in range(chips):
            part = pl.ds(pl.multiple_of((2 * k + owner_core) * rows, rows), rows)
            term = shares(part, windows_of(part))
            total = term if total is None else total + term
        if extra:
            part = slice(owners * rows, owners * rows + here)
            total += shares(part, windows_of(part))
        return total

    def merge(total):
        count = bins // LANES
        sums = [None] * count
        lanes = iota((blocks * cells, LANES), 1)
        for d in range(slabs):
            first = d * bins_here - front
            turn = first % LANES
            low = first // LANES
            window = total[:, d * LANES : (d + 1) * LANES]
            if turn:
                window = pltpu.roll(window, turn, 1)
            for n, keep in ((low, lanes >= turn), (low + 1, lanes < turn)):
                if 0 <= n < count:
                    piece = jnp.where(keep, window, 0.0)
                    sums[n] = piece if sums[n] is None else sums[n] + piece
        for n in range(count):
            grad_ref[:, n * LANES : (n + 1) * LANES] = sums[n].astype(BF16)

    def cot_edges():
        @pl.when(has_prev)
        def _():
            cot_up().wait_recv()

        @pl.when(has_next)
        def _():
            cot_down().wait_recv()

    def first_grads():
        total_ref[...] = grads(core, False)

    def last_grads():
        merge(total_ref[...] + grads(1 - core, True))

    def finish():
        for k in range(chips):
            core_copy(k).wait_send()
        if mid > 1:
            sent(zsend_ref.at[0 : mid - 1], z_s.at[0])
        sent(zsend_ref.at[0:mid], z_s.at[3])

        @pl.when(is_gate)
        def _():
            sent(zsend_ref.at[0:mid], z_s.at[2])
            for j in range(1, mid):
                sent(zsend_ref.at[0:mid], gr_s.at[j - 1])

        @pl.when(jnp.logical_not(is_gate))
        def _():
            sent(zsend_ref.at[0:mid], z_s.at[1])

        for side in range(2):

            @pl.when(edges(side))
            def _():
                sent(hrecv_ref.at[side, 0:mid], h_s.at[side])

            @pl.when(edges(side) & is_gate)
            def _():
                sent(hrecv_ref.at[side, 0:mid], h_s.at[2 + side])

        for j in range(1, chips):
            for p in range(2):
                x_copy(j, p).wait_send()
            sent(every_ref.at[:, 0:rows], gx_s.at[j - 1])
        sent(every_ref.at[:, 0 : chips * rows], gc_s.at[0])

        @pl.when(has_prev)
        def _():
            cot_down().wait_send()

        @pl.when(has_next)
        def _():
            cot_up().wait_send()

    green(0, 0)
    own_parts()
    core_sums()
    third_round()
    send_windows(2)
    green(1, 0)
    green(2, 0)
    loads[6].wait()
    cot_edges()
    backward(0)
    backward(1)
    all_here()
    gate_sums(2)
    core_copy(chip).wait_recv()
    sum_and_send(0)
    backward(2)
    relay(0)
    sum_and_send(1)
    spread_bins(z, 0)
    spread_bins(z, 1)
    relay(1)
    near_bins(0)
    near_bins(1)
    turn_shares()
    green(2, 1)
    gate_sums(0)
    green(0, 1)
    green(1, 1)
    gate_sums(1)
    relay(2)
    forward(2)
    far_bins(0)
    far_bins(1)
    pass_bins(0)
    forward(0)
    pass_bins(1)
    first_grads()
    forward(1)
    near_bins(2)
    far_bins(2)
    core_bins()
    last_grads()
    finish()


def store_kernel(signal_ref, grad_ref, signal_out, grad_out, sems):
    copies = (
        pltpu.make_async_copy(signal_ref, signal_out, sems.at[0]),
        pltpu.make_async_copy(grad_ref, grad_out, sems.at[1]),
    )
    for copy in copies:
        copy.start()
    for copy in copies:
        copy.wait()


def local(charge, intersection, ovl_block, ovl_count, diff_class, response, cotangent):
    blocks, planes, entries, wires, cells = intersection.shape
    bins = charge.shape[1]
    owners, slabs = lax.axis_size("gz"), lax.axis_size("drift")
    here, ticks_here = cotangent.shape[1:]
    spread, length = response.shape[1:]
    chips = owners // 2
    rows = 2 * here
    bins_here = bins // slabs
    block = math.gcd(ticks_here, 2 * LANES)
    pairs = (spread + 1) // 2
    front = (length - 1 + REACH + (TPB - 1) // 2) // TPB
    while (LOW - TPB * front) % LANES >= TPB:
        front += 1
    taps_rows = round_up(2 * pairs, 8)
    depth = round_up(length, ROWS)
    assert owners % 2 == 0 and slabs % 2 == 0 and planes == 3
    assert front + bins_here + HB <= LANES
    assert block * (ticks_here // block - 1) // TPB + WIN <= LANES
    assert length - 1 + REACH + (TPB - 1) // 2 - LOW < 2 * LANES
    dma = pltpu.SemaphoreType.DMA
    others = max(chips - 1, 1)
    mid = slabs // 2
    signal, charge_grad = pl.pallas_call(
        functools.partial(kernel, (owners, slabs, front, pairs, block)),
        out_shape=(
            jax.ShapeDtypeStruct((planes, here, ticks_here), BF16),
            jax.ShapeDtypeStruct((blocks * cells, bins), BF16),
        ),
        in_specs=[HBM] * 7,
        out_specs=(VMEM, VMEM),
        scratch_shapes=[
            pltpu.SMEM((planes, entries, blocks), jnp.int32),
            pltpu.SMEM(ovl_count.shape, jnp.int32),
            pltpu.VMEM(charge.shape, BF16),
            pltpu.VMEM(intersection.shape, BF16),
            pltpu.VMEM(diff_class.shape, jnp.int32),
            pltpu.VMEM(response.shape, BF16),
            pltpu.VMEM(cotangent.shape, BF16),
            dma((7,)),
            pltpu.SemaphoreType.REGULAR((2,)),
            pltpu.VMEM((owners * rows + here, blocks * cells), BF16),
            pltpu.VMEM((chips, rows, bins), F32),
            pltpu.VMEM((chips, rows, bins), BF16),
            pltpu.VMEM((chips, rows, bins), BF16),
            pltpu.VMEM((others, 2, here, bins), BF16),
            pltpu.VMEM((others, 2, here, bins), BF16),
            pltpu.VMEM((bins, slabs * LANES), BF16),
            pltpu.VMEM((slabs, planes, here, LANES), BF16),
            pltpu.VMEM((mid, planes, here, LANES), BF16),
            pltpu.VMEM((max(mid - 1, 1), mid, planes, here, LANES), BF16),
            pltpu.VMEM((mid, planes, here, LANES), BF16),
            pltpu.VMEM((2, mid + 1, planes, ROWS, LANES), BF16),
            pltpu.VMEM((2, planes, ROWS, ticks_here), BF16),
            pltpu.VMEM((slabs, owners * rows + here, LANES), BF16),
            pltpu.VMEM((blocks * cells, owners * rows + here), BF16),
            pltpu.VMEM((planes, taps_rows, depth), F32),
            pltpu.VMEM((2, planes * taps_rows * (NDIFF + 2), LANES), F32),
            pltpu.VMEM((2, planes, 2 * pairs, LANES, 4 * LANES), BF16),
            pltpu.VMEM((here + 2 * ROWS, 2 * pairs * WIN), F32),
            pltpu.VMEM((planes, here + 2 * ROWS + 8, LANES), F32),
            pltpu.VMEM((here + 2 * ROWS, LANES), F32),
            pltpu.VMEM((blocks * cells, slabs * LANES), F32),
            dma((chips,)),
            dma((chips,)),
            dma((others, 2)),
            dma((others, 2)),
            dma((4,)),
            dma((mid, planes)),
            dma((max(mid - 1, 1), planes)),
            dma((4,)),
            dma((2, planes)),
            dma((2,)),
            dma((2,)),
            dma((slabs, planes)),
            dma((max(mid - 1, 1),)),
            dma((others,)),
            dma((others, slabs, 2)),
            dma((2,)),
        ],
        compiler_params=pltpu.CompilerParams(
            collective_id=0, has_side_effects=True, vmem_limit_bytes=LIMIT * 1024 * 1024
        ),
        name="planes",
    )(
        *(
            pltpu.with_memory_space_constraint(array, pltpu.HBM)
            for array in (
                jnp.transpose(ovl_block, (1, 2, 0)),
                ovl_count,
                charge,
                intersection,
                diff_class,
                response,
                cotangent,
            )
        ),
    )
    return pl.pallas_call(
        store_kernel,
        out_shape=(
            jax.ShapeDtypeStruct(signal.shape, BF16),
            jax.ShapeDtypeStruct(charge_grad.shape, BF16),
        ),
        in_specs=[VMEM, VMEM],
        out_specs=(HBM, HBM),
        scratch_shapes=[pltpu.SemaphoreType.DMA((2,))],
        compiler_params=pltpu.CompilerParams(vmem_limit_bytes=4 * 1024 * 1024),
        name="store",
    )(signal, charge_grad)


def solution(mesh):
    return jax.shard_map(
        local,
        mesh=mesh,
        in_specs=(
            P(("apa", "gz", "drift"), None),
            P(("apa", "gz", "drift"), None, None, None, None),
            P(("apa", "gz", "drift"), None, None),
            P(("apa", "gz", "drift"), None),
            P("apa"),
            P(),
            P("apa", "gz", "drift"),
        ),
        out_specs=(P("apa", "gz", "drift"), P(("apa", "gz", "drift"), None)),
        check_vma=False,
    )
```

profile of v0, /device:TPU:0, one launch (start us, length us, event | category | flops | bytes accessed | tf_op | source)
XLA Modules:
  0.0 29.9 jit_solution(18177795675434613360)
XLA Ops:
  0.6 28.2 %planes.1 = (bf16[3,128,768]{2,1,0:T(8,128)(2,1)S(1)}, bf16[512,384]{1,0:T(8,128)(2,1)S(1)}) custom-call(s32[3,2,4]{2,1,0:T(2,128)} %bitcast.1, s32[4,3]{1,0:T(4,128)} %cnt_hbm.1, bf16[512,384]{1,0:T(8,128)(2,1)} %charge_hbm.1, bf16[4,3,2,32,128]{4,3,2,1,0:T(8,128)(2,1)} %inter_hbm.1, s32[384]{0:T(512)} %class_hbm.1, bf16[3,21,200]{2,1,0:T(8,128)(2,1)} %resp_hbm.1, ...), custom_call_target="tpu_custom_call" | custom-call | tf_op jit(solution)/shard_map/planes/pallas_call | solution.py:868
  28.8 1.0 %store.1 = (bf16[3,128,768]{2,1,0:T(8,128)(2,1)}, bf16[512,384]{1,0:T(8,128)(2,1)}) custom-call(bf16[3,128,768]{2,1,0:T(8,128)(2,1)S(1)} %get-tuple-element.4.signal_ref, bf16[512,384]{1,0:T(8,128)(2,1)S(1)} %get-tuple-element.5.grad_ref), custom_call_target="tpu_custom_call" | custom-call | tf_op jit(solution)/shard_map/store/pallas_call | solution.py:943
where the time goes:
time: 30.1 us; the launch traced here: 29.9 us
  Pallas kernels  29.1 us (97%)
  between operations  0.8 us (3%)
    pallas_call x1, Pallas kernels, local(): pl.pallas_call(functools.partial(kernel, (owners, slabs, front, pairs, bl...  28.2 us
    pallas_call x1, Pallas kernels, local(): pl.pallas_call(store_kernel, out_shape=(jax.ShapeDtypeStruct(signal.shape...  0.96 us

commit v1 on v0

--- a/solution.py
+++ b/solution.py
@@ -407,9 +407,23 @@
         return base + (z - base + j) % mid
 
     def frame(p, sums):
-        framed = dot(sums.astype(BF16), place_ref[...]).astype(BF16)
+        level = jnp.mean(sums, axis=1, keepdims=True).astype(BF16)
+        framed = dot((sums - level.astype(F32)).astype(BF16), place_ref[...])
         for d in range(slabs):
-            zsend_ref[d, p] = framed[:, d * LANES : (d + 1) * LANES]
+            zsend_ref[d, p] = with_level(framed[:, d * LANES : (d + 1) * LANES], level)
+
+    def with_level(window, upper, lower=0.0):
+        at = iota(window.shape, 1)
+        window = jnp.where(at == 0, upper.astype(F32), window)
+        return jnp.where(at == 1, lower, window).astype(BF16)
+
+    def level_of(window):
+        return window[:, 0:1] + window[:, 1:2]
+
+    def leveled(window):
+        bin_here = iota(window.shape, 1) + bins_here * z - front
+        known = (bin_here >= 0) & (bin_here < bins)
+        return jnp.where(known, window + level_of(window), 0.0)
 
     def half_copy(j, p):
         return remote(
@@ -498,7 +512,9 @@
                 total = zsend_ref[base_there + i, p].astype(F32)
                 for n in range(mid - 1):
                     total += zgate_ref[n, i, p].astype(F32)
-                zsum_ref[i, p] = total.astype(BF16)
+                level = level_of(total)
+                upper = level.astype(BF16)
+                zsum_ref[i, p] = with_level(total, upper, level - upper.astype(F32))
                 sum_copy(i, p).start()
             for side in range(2):
 
@@ -659,7 +675,7 @@
             total += zrecv_ref[j - 1, p].astype(F32)
         sum_copy(0, p).wait_recv()
         total += zrecv_ref[mid - 1, p].astype(F32)
-        field_ref[p, ROWS : ROWS + here, :] = total
+        field_ref[p, ROWS : ROWS + here, :] = leveled(total)
 
     tall = here + 2 * ROWS
     used = tall
@@ -677,7 +693,7 @@
             edge = hrecv_ref[side, 0, p].astype(F32)
             for j in range(1, mid + 1):
                 edge += hrecv_ref[side, j, p].astype(F32)
-            field_ref[p, at : at + ROWS, :] = edge
+            field_ref[p, at : at + ROWS, :] = leveled(edge)
         for c in range(chunks):
             first = block * c // TPB
             this = field_ref[p, 0:used, :]
@@ -819,8 +835,8 @@
     forward(2)
     far_bins(0)
     far_bins(1)
+    forward(0)
     pass_bins(0)
-    forward(0)
     pass_bins(1)
     first_grads()
     forward(1)
@@ -854,12 +870,13 @@
     block = math.gcd(ticks_here, 2 * LANES)
     pairs = (spread + 1) // 2
     front = (length - 1 + REACH + (TPB - 1) // 2) // TPB
+    least = front
     while (LOW - TPB * front) % LANES >= TPB:
         front += 1
     taps_rows = round_up(2 * pairs, 8)
     depth = round_up(length, ROWS)
     assert owners % 2 == 0 and slabs % 2 == 0 and planes == 3
-    assert front + bins_here + HB <= LANES
+    assert front - least >= 2 and front + bins_here + HB <= LANES
     assert block * (ticks_here // block - 1) // TPB + WIN <= LANES
     assert length - 1 + REACH + (TPB - 1) // 2 - LOW < 2 * LANES
     dma = pltpu.SemaphoreType.DMA

time: 30.1 us -> 30 us (level)
  no operation moved by 1% of the time
where the time goes in v1:
time: 30 us; the launch traced here: 29.8 us
  Pallas kernels  29 us (97%)
  between operations  0.8 us (3%)
    pallas_call x1, Pallas kernels, local(): pl.pallas_call(functools.partial(kernel, (owners, slabs, front, pairs, bl...  28 us
    pallas_call x1, Pallas kernels, local(): pl.pallas_call(store_kernel, out_shape=(jax.ShapeDtypeStruct(signal.shape...  0.96 us

profile of v1, /device:TPU:0, one launch (start us, length us, event | category | flops | bytes accessed | tf_op | source)
XLA Modules:
  0.0 29.8 jit_solution(14910193614878767298)
XLA Ops:
  0.6 28.0 %planes.1 = (bf16[3,128,768]{2,1,0:T(8,128)(2,1)S(1)}, bf16[512,384]{1,0:T(8,128)(2,1)S(1)}) custom-call(s32[3,2,4]{2,1,0:T(2,128)} %bitcast.1, s32[4,3]{1,0:T(4,128)} %cnt_hbm.1, bf16[512,384]{1,0:T(8,128)(2,1)} %charge_hbm.1, bf16[4,3,2,32,128]{4,3,2,1,0:T(8,128)(2,1)} %inter_hbm.1, s32[384]{0:T(512)} %class_hbm.1, bf16[3,21,200]{2,1,0:T(8,128)(2,1)} %resp_hbm.1, ...), custom_call_target="tpu_custom_call" | custom-call | tf_op jit(solution)/shard_map/planes/pallas_call | solution.py:885
  28.6 1.0 %store.1 = (bf16[3,128,768]{2,1,0:T(8,128)(2,1)}, bf16[512,384]{1,0:T(8,128)(2,1)}) custom-call(bf16[3,128,768]{2,1,0:T(8,128)(2,1)S(1)} %get-tuple-element.4.signal_ref, bf16[512,384]{1,0:T(8,128)(2,1)S(1)} %get-tuple-element.5.grad_ref), custom_call_target="tpu_custom_call" | custom-call | tf_op jit(solution)/shard_map/store/pallas_call | solution.py:960

commit v2 on v1

--- a/solution.py
+++ b/solution.py
@@ -756,10 +756,10 @@
             cot_down().wait_recv()
 
     def first_grads():
-        total_ref[...] = grads(core, False)
+        total_ref[...] = grads(core, True)
 
     def last_grads():
-        merge(total_ref[...] + grads(1 - core, True))
+        merge(total_ref[...] + grads(1 - core, False))
 
     def finish():
         for k in range(chips):
@@ -838,10 +838,10 @@
     forward(0)
     pass_bins(0)
     pass_bins(1)
+    near_bins(2)
+    far_bins(2)
     first_grads()
     forward(1)
-    near_bins(2)
-    far_bins(2)
     core_bins()
     last_grads()
     finish()

time: 30 us -> 29.8 us (level)
  no operation moved by 1% of the time
where the time goes in v2:
time: 29.8 us; the launch traced here: 29.6 us
  Pallas kernels  28.8 us (97%)
  between operations  0.8 us (3%)
    pallas_call x1, Pallas kernels, local(): pl.pallas_call(functools.partial(kernel, (owners, slabs, front, pairs, bl...  27.9 us
    pallas_call x1, Pallas kernels, local(): pl.pallas_call(store_kernel, out_shape=(jax.ShapeDtypeStruct(signal.shape...  0.96 us

profile of v2, /device:TPU:0, one launch (start us, length us, event | category | flops | bytes accessed | tf_op | source)
XLA Modules:
  0.0 29.6 jit_solution(2841640771319803504)
XLA Ops:
  0.6 27.9 %planes.1 = (bf16[3,128,768]{2,1,0:T(8,128)(2,1)S(1)}, bf16[512,384]{1,0:T(8,128)(2,1)S(1)}) custom-call(s32[3,2,4]{2,1,0:T(2,128)} %bitcast.1, s32[4,3]{1,0:T(4,128)} %cnt_hbm.1, bf16[512,384]{1,0:T(8,128)(2,1)} %charge_hbm.1, bf16[4,3,2,32,128]{4,3,2,1,0:T(8,128)(2,1)} %inter_hbm.1, s32[384]{0:T(512)} %class_hbm.1, bf16[3,21,200]{2,1,0:T(8,128)(2,1)} %resp_hbm.1, ...), custom_call_target="tpu_custom_call" | custom-call | tf_op jit(solution)/shard_map/planes/pallas_call | solution.py:885
  28.5 1.0 %store.1 = (bf16[3,128,768]{2,1,0:T(8,128)(2,1)}, bf16[512,384]{1,0:T(8,128)(2,1)}) custom-call(bf16[3,128,768]{2,1,0:T(8,128)(2,1)S(1)} %get-tuple-element.4.signal_ref, bf16[512,384]{1,0:T(8,128)(2,1)S(1)} %get-tuple-element.5.grad_ref), custom_call_target="tpu_custom_call" | custom-call | tf_op jit(solution)/shard_map/store/pallas_call | solution.py:960
